TPU v7x, 32 devices: a whole 2x2x4 slice. The times are simulated.
32 devices in a mesh: groups: 2 (over x), tile: 16 (over z, y, core).
Axes of the slice: x: 2, y: 2, z: 4, core: 2. Of those that a mesh axis runs over, the one named last changes fastest.
Arguments:
- grid_tokens: bfloat16 [16384, 512], P(('groups', 'tile')), parts along dimension 0, may hold values from -220 to 220
- obs_features: bfloat16 [65536, 128], P(('groups', 'tile')), parts along dimension 0, may hold values from -45 to 45
- w_obs: bfloat16 [128, 512], replicated, may hold values from -0.5 to 0.5
- b_obs: float32 [512], replicated, may hold values from -4 to 4
- w_query: bfloat16 [512, 512], replicated, may hold values from -0.25 to 0.25
- w_key: bfloat16 [512, 512], replicated, may hold values from -0.25 to 0.25
- w_value: bfloat16 [512, 512], replicated, may hold values from -0.25 to 0.25
- w_out: bfloat16 [512, 512], replicated, may hold values from -0.25 to 0.25
- block_lists: int32 [128, 32], P('groups'), parts along dimension 0, may hold values from 0 to 511, as said below
- block_counts: int32 [128], P('groups'), parts along dimension 0, may hold values from 24 to 32, as said below
- block_position: int32 [1024], P('groups'), parts along dimension 0, may hold values from 0 to 511, as said below
- proc_order: int32 [128], P('groups'), parts along dimension 0, may hold values from 0 to 63, each once
Outputs:
- arranged: bfloat16 [16384, 512], P(('groups', 'tile')), parts along dimension 0
There are 2 independent parts, one for each index of `groups`. A program takes and returns all parts, laid end to end along the dimension named above; an argument that names none is the same for every part. Nothing has to cross between parts.
Inputs may be any that keep to these rules, and one draw needn't show every extreme that they name: `block_lists`: over the entries below block_counts of the 4 tiles t of one device (t // 4 equal), at most 16 name blocks whose storage position // 32 is any one device; in every draw some device has exactly 16 from some device. `block_counts`: some tile uses all 32 entries. `block_position`: A permutation of the storage positions.
All inputs are finite; a program needn't handle non-finite values.
Results may differ from a plain program's by a relative error of at most 0.012.
The roundings to bfloat16 on the way count: a program that leaves them out, or rounds other values in their place, can miss the bound.
Values may be sent and summed in bfloat16 or wider, within the bound.
A program may use at most 128 MiB of HBM per device.

v0:
```python
import jax
import jax.numpy as jnp
from jax import lax
from jax.sharding import PartitionSpec as P

HEADS = 8
BLOCK = 64
NSEL = 32
TILE_ROWS = 128


def embed_rows(feats, feat_mean, feat_rstd, w_obs, b_obs):
    normed = ((feats.astype(jnp.float32) - feat_mean) * feat_rstd).astype(jnp.bfloat16)
    hidden = jnp.dot(normed, w_obs, preferred_element_type=jnp.float32) + b_obs
    return jax.nn.gelu(hidden, approximate=True).astype(jnp.bfloat16)


def local(
    grid_tokens,
    obs_features,
    w_obs,
    b_obs,
    w_query,
    w_key,
    w_value,
    w_out,
    block_lists,
    block_counts,
    block_position,
    proc_order,
):
    tile_count = lax.axis_size("tile")
    own_index = lax.axis_index("tile")
    obs_blocks = obs_features.shape[0] // BLOCK
    tile_local = grid_tokens.shape[0] // TILE_ROWS
    entry_count = tile_local * NSEL
    capacity = max(2, 2 * entry_count // tile_count)
    width = grid_tokens.shape[1]
    obs_wide = obs_features.astype(jnp.float32)
    first_sum, second_sum = lax.psum(
        (jnp.sum(obs_wide, axis=0), jnp.sum(obs_wide * obs_wide, axis=0)), "tile"
    )
    obs_total = obs_features.shape[0] * tile_count
    feat_mean = first_sum / obs_total
    feat_rstd = lax.rsqrt(second_sum / obs_total - feat_mean * feat_mean + 1e-05)
    spots = jnp.take(block_position, block_lists, axis=0)
    is_valid = jnp.arange(NSEL, dtype=jnp.int32)[None, :] < block_counts[:, None]
    owner_dev = (spots // obs_blocks).reshape(tile_count, entry_count)
    local_blk = (spots % obs_blocks).reshape(tile_count, entry_count)
    valid_rows = is_valid.reshape(tile_count, entry_count)
    entry_order = jnp.arange(entry_count, dtype=jnp.int32)
    earlier = (
        (owner_dev[:, :, None] == owner_dev[:, None, :])
        & valid_rows[:, None, :]
        & (entry_order[None, :] < entry_order[:, None])[None, :, :]
    )
    slot_rank = jnp.sum(earlier.astype(jnp.int32), axis=2)
    mine = valid_rows & (owner_dev == own_index)
    slot_ids = jnp.arange(capacity, dtype=jnp.int32)
    hits = mine[:, None, :] & (slot_rank[:, None, :] == slot_ids[None, :, None])
    present = jnp.any(hits, axis=2)
    slot_block = jnp.sum(jnp.where(hits, local_blk[:, None, :], 0), axis=2)
    my_owner = lax.dynamic_index_in_dim(owner_dev, own_index, 0, keepdims=False)
    my_rank = lax.dynamic_index_in_dim(slot_rank, own_index, 0, keepdims=False)
    my_valid = lax.dynamic_index_in_dim(valid_rows, own_index, 0, keepdims=False)
    pick_slot = jnp.where(my_valid, my_owner * capacity + my_rank, 0)
    raw_blocks = obs_features.reshape(obs_blocks, BLOCK, obs_features.shape[1])
    chosen = jnp.take(raw_blocks, slot_block, axis=0)
    incoming = lax.all_to_all(
        jnp.where(present[:, :, None, None], chosen, jnp.zeros((), raw_blocks.dtype)),
        "tile",
        split_axis=0,
        concat_axis=0,
        tiled=True,
    )
    flat_blocks = incoming.reshape(tile_count * capacity, BLOCK, incoming.shape[3])
    chosen_rows = embed_rows(
        jnp.take(flat_blocks, pick_slot, axis=0).reshape(entry_count * BLOCK, incoming.shape[3]),
        feat_mean,
        feat_rstd,
        w_obs,
        b_obs,
    )
    key_rows = jnp.dot(chosen_rows, w_key, preferred_element_type=jnp.float32).astype(jnp.bfloat16)
    value_rows = jnp.dot(chosen_rows, w_value, preferred_element_type=jnp.float32).astype(
        jnp.bfloat16
    )
    query_rows = jnp.dot(grid_tokens, w_query, preferred_element_type=jnp.float32).astype(
        jnp.bfloat16
    )
    my_counts = lax.dynamic_slice_in_dim(block_counts, own_index * tile_local, tile_local)
    head_dim = width // HEADS
    scale = 1.0 / head_dim**0.5
    key_span = NSEL * BLOCK
    results = []
    for tile_pos in range(tile_local):
        query_tile = query_rows[tile_pos * TILE_ROWS : (tile_pos + 1) * TILE_ROWS]
        key_tile = key_rows[tile_pos * key_span : (tile_pos + 1) * key_span]
        value_tile = value_rows[tile_pos * key_span : (tile_pos + 1) * key_span]
        keymask = jnp.repeat(jnp.arange(NSEL, dtype=jnp.int32) < my_counts[tile_pos], BLOCK)

        def one_head(
            head, query_tile=query_tile, key_tile=key_tile, value_tile=value_tile, keymask=keymask
        ):
            query_head = lax.dynamic_slice_in_dim(query_tile, head * head_dim, head_dim, 1)
            key_head = lax.dynamic_slice_in_dim(key_tile, head * head_dim, head_dim, 1)
            value_head = lax.dynamic_slice_in_dim(value_tile, head * head_dim, head_dim, 1)
            scores = (
                lax.dot_general(
                    query_head,
                    key_head,
                    (((1,), (1,)), ((), ())),
                    preferred_element_type=jnp.float32,
                )
                * scale
            )
            scores = jnp.where(keymask[None, :], scores, jnp.float32(-1e30))
            peak = jnp.max(scores, axis=-1, keepdims=True)
            expo = jnp.exp(scores - peak)
            totals = jnp.sum(expo, axis=-1, keepdims=True)
            weights_bf = expo.astype(jnp.bfloat16)
            return jnp.dot(weights_bf, value_head, preferred_element_type=jnp.float32) / totals

        per_head = lax.map(one_head, jnp.arange(HEADS, dtype=jnp.int32))
        results.append(
            jnp.transpose(per_head, (1, 0, 2)).reshape(TILE_ROWS, width).astype(jnp.bfloat16)
        )
    attended = jnp.concatenate(results, axis=0)
    encoded = jnp.dot(attended, w_out, preferred_element_type=jnp.float32).astype(jnp.bfloat16)
    outgoing = encoded.reshape(tile_local, tile_count, TILE_ROWS // tile_count, width)
    arrived = lax.all_to_all(outgoing, "tile", split_axis=1, concat_axis=0, tiled=True)
    arrived = arrived.reshape(tile_count * tile_local, TILE_ROWS // tile_count, width)
    return jnp.take(arrived, proc_order, axis=0).reshape(
        tile_count * tile_local * (TILE_ROWS // tile_count), width
    )


def solution(mesh):
    in_specs = (
        P(("groups", "tile"), None),
        P(("groups", "tile"), None),
        P(),
        P(),
        P(),
        P(),
        P(),
        P(),
        P("groups", None),
        P("groups"),
        P("groups"),
        P("groups"),
    )
    out_specs = P(("groups", "tile"), None)
    return jax.shard_map(local, mesh=mesh, in_specs=in_specs, out_specs=out_specs, check_vma=False)
```

profile of v0, /device:TPU:0, one launch (start us, length us, event | category | flops | bytes accessed | tf_op | source)
XLA Modules:
  0.0 354.2 jit_solution(3823423452104202265)
XLA Ops:
  1.0 13.2 %gather_fusion = s32[2048]{0:T(1024)S(1)} fusion(s32[512]{0:T(512)S(1)} %copy-done.2, s32[2048]{0:T(1024)S(1)} %broadcast_clamp_fusion), kind=kCustom, calls=%fused_computation | custom fusion | bytes 24576 | tf_op jit(solution)/shard_map/jit(_take)/gather | solution.py:46
  16.2 3.1 gather_fusion.1
  19.3 3.9 %select_select_fusion = bf16[16,16,64,128]{3,2,1,0:T(8,128)(2,1)} fusion(bf16[16,16,64,128]{3,2,1,0:T(8,128)(2,1)} %bitcast.84, pred[16,16]{1,0:T(8,128)(4,1)S(1)} %compare_and_fusion, pred[16,16]{1,0:T(8,128)(4,1)S(1)} %fusion.75), kind=kLoop, calls=%fused_computation.76 | loop fusion | flops 4194304 | bytes 8389120 | tf_op jit(solution)/shard_map/jit(_where)/select_n | solution.py:70
  23.2 7.6 %all-to-all-start = ((bf16[16,16,64,128]{3,2,1,0:T(8,128)(2,1)}), bf16[16,16,64,128]{3,2,1,0:T(8,128)(2,1)}, u32[]{:S(2)}, u32[]{:S(2)}) async-start(bf16[16,16,64,128]{3,2,1,0:T(8,128)(2,1)} %select_select_fusion), calls=%async_computation | async-start | bytes 8388608 | tf_op jit(solution)/shard_map/all_to_all | solution.py:69
  31.4 95.8 %all-reduce = (f32[128]{0:T(128)S(1)}, f32[128]{0:T(128)S(1)}) all-reduce(f32[128]{0:T(128)S(1)} %get-tuple-element.226, f32[128]{0:T(128)S(1)} %get-tuple-element.225), channel_id=1, replica_groups=mesh['groups'=2,'tile'=16] {'tile'}, use_global_device_ids=true, to_apply=%region_6.7 | all-reduce | flops 256 | bytes 2048 | tf_op jit(solution)/shard_map/psum | solution.py:40
  130.8 3.2 gather_fusion.2
  134.0 4.3 %bitcast_select_fusion = bf16[8192,128]{1,0:T(8,128)(2,1)S(1)} fusion(bf16[128,64,128]{2,1,0:T(8,128)(2,1)S(1)} %gather_fusion.2, pred[8192]{0:T(1024)(128)(4,1)S(1)} %broadcast_in_dim.178), kind=kLoop, calls=%fused_computation.77 | loop fusion | flops 1048576 | bytes 4202496 | tf_op jit(solution)/shard_map/jit(_take)/select_n | solution.py:78
  138.3 6.6 %fusion.63 = bf16[8192,512]{1,0:T(8,128)(2,1)S(1)} fusion(bf16[128,512]{1,0:T(8,128)(2,1)S(1)} %copy-done.8, f32[512]{0:T(512)S(1)} %copy-done.9, bf16[8192,128]{1,0:T(8,128)(2,1)S(1)} %bitcast_select_fusion, f32[128]{0:T(128)S(1)} %get-tuple-element.315, f32[128]{0:T(128)S(1)} %get-tuple-element.314), kind=kOutput, calls=%fused_computation.72 | convolution fusion | flops 1119879168 | bytes 10619904 | tf_op jit(solution)/shard_map/dot_general | solution.py:14
  144.9 3.2 copy-done.11
  148.1 4.7 %convolution_convert_fusion = bf16[8192,512]{1,0:T(8,128)(2,1)S(1)} fusion(bf16[8192,512]{1,0:T(8,128)(2,1)S(1)} %fusion.63, bf16[512,512]{1,0:T(8,128)(2,1)S(1)} %copy-done), kind=kOutput, calls=%fused_computation.73 | convolution fusion | flops 4299161600 | bytes 17301504 | tf_op jit(solution)/shard_map/dot_general | solution.py:85
  152.9 8.1 %convolution_convert_fusion.1 = bf16[8192,512]{1,0:T(8,128)(2,1)S(1)} fusion(bf16[8192,512]{1,0:T(8,128)(2,1)} %copy-done.11, bf16[512,512]{1,0:T(8,128)(2,1)S(1)} %copy-done.7), kind=kOutput, calls=%fused_computation.74 | convolution fusion | flops 4299161600 | bytes 17301504 | tf_op jit(solution)/shard_map/dot_general | solution.py:84
  161.0 5.2 %fusion.86 = (bf16[2048,512]{1,0:T(8,128)(2,1)}, bf16[2048,512]{1,0:T(8,128)(2,1)S(1)}, bf16[2048,512]{1,0:T(8,128)(2,1)}, bf16[2048,512]{1,0:T(8,128)(2,1)}, bf...) fusion(bf16[8192,512]{1,0:T(8,128)(2,1)S(1)} %convolution_conver, ...), kind=kLoop, calls=%fused_computation.140 | loop fusion | bytes 33554432 | tf_op jit(solution)/shard_map/slice | solution.py:99
  166.2 40.6 %while.44 = (s32[]{:T(128)}, bf16[8,128,64]{1,2,0:T(8,128)(2,1)S(1)}, s32[8]{0:T(128)S(1)}, bf16[128,512]{1,0:T(8,128)(2,1)S(1)}, bf16[2048,512]{1,0:T(8,128)(2,...) while((s32[]{:T(128)}, ...), condition=%wide.region_10.11_spmd.clone, body=%wide.region_7.10_spmd.clone.sunk | while | flops 68951808 | bytes 4272331 | solution.py:124
  169.6 1.7 fusion.122
  174.7 1.7 fusion.122
  184.8 1.7 fusion.122
  189.9 1.7 fusion.122
  194.9 1.7 fusion.122
  206.8 40.2 %while.45 = (s32[]{:T(128)}, bf16[8,128,64]{1,2,0:T(8,128)(2,1)S(1)}, s32[8]{0:T(128)S(1)}, bf16[128,512]{1,0:T(8,128)(2,1)S(1)}, bf16[2048,512]{1,0:T(8,128)(2,...) while((s32[]{:T(128)}, ...), condition=%wide.region_14.15_spmd.clone, body=%wide.region_11.14_spmd.clone.sunk | while | flops 68951808 | bytes 4272331 | solution.py:124
  210.1 1.7 fusion.127
  247.1 39.2 %while.46 = (s32[]{:T(128)}, bf16[8,128,64]{1,2,0:T(8,128)(2,1)S(1)}, s32[8]{0:T(128)S(1)}, bf16[128,512]{1,0:T(8,128)(2,1)S(1)}, bf16[2048,512]{1,0:T(8,128)(2,...) while((s32[]{:T(128)}, ...), condition=%wide.region_18.19_spmd.clone, body=%wide.region_15.18_spmd.clone.sunk | while | flops 68951808 | bytes 4272331 | solution.py:124
  250.5 1.7 fusion.132
  255.4 1.7 fusion.132
  260.2 1.7 fusion.132
  265.1 1.7 fusion.132
  270.0 1.7 fusion.132
  274.9 1.7 fusion.132
  279.7 1.7 fusion.132
  284.6 1.7 fusion.132
  286.4 31.1 %while.47 = (s32[]{:T(128)}, bf16[8,128,64]{1,2,0:T(8,128)(2,1)S(1)}, s32[8]{0:T(128)S(1)}, bf16[128,512]{1,0:T(8,128)(2,1)S(1)}, bf16[2048,512]{1,0:T(8,128)(2,...) while((s32[]{:T(128)}, ...), condition=%wide.region_22.23_spmd.clone, body=%wide.region_19.22_spmd.clone.sunk | while | flops 68951808 | bytes 4271823 | solution.py:124
  319.9 18.5 %all-to-all-start.1 = ((bf16[4,16,8,512]{3,2,0,1:T(8,128)(2,1)}), bf16[4,16,8,512]{3,2,0,1:T(8,128)(2,1)S(1)}, u32[]{:S(2)}, u32[]{:S(2)}) async-start(bf16[4,16,8,512]{3,2,0,1:T(8,128)(2,1)} %copy.20), calls=%async_computation.1 | async-start | bytes 1048576 | tf_op jit(solution)/shard_map/all_to_all | solution.py:131
  338.6 14.0 %all-to-all-done.1 = bf16[4,16,8,512]{3,2,0,1:T(8,128)(2,1)S(1)} async-done(((bf16[4,16,8,512]{3,2,0,1:T(8,128)(2,1)}), bf16[4,16,8,512]{3,2,0,1:T(8,128)(2,1)S(1)}, u32[]{:S(2)}, u32[]{:S(2)}) %all-to-all-start.1) | async-done | bytes 524320 | tf_op jit(solution)/shard_map/all_to_all | solution.py:131
  (256 shorter events, 116.8 us)
Async XLA Ops:
  0.0 148.1 %copy-start = (bf16[512,512]{1,0:T(8,128)(2,1)S(1)}, bf16[512,512]{1,0:T(8,128)(2,1)}, u32[]{:S(2)}) copy-start(bf16[512,512]{1,0:T(8,128)(2,1)} %param.26) | copy-start | bytes 1572868
  0.0 1.0 copy-start.2
  1.0 13.4 %copy-start.6 = (s32[64]{0:T(128)S(1)}, s32[64]{0:T(128)}, u32[]{:S(2)}) copy-start(s32[64]{0:T(128)} %param.29) | copy-start | bytes 772
  1.0 15.2 %copy-start.3 = (bf16[2048,128]{1,0:T(8,128)(2,1)S(1)}, bf16[2048,128]{1,0:T(8,128)(2,1)}, u32[]{:S(2)}) copy-start(bf16[2048,128]{1,0:T(8,128)(2,1)} %param.21) | copy-start | bytes 1572868
  23.2 107.1 %copy-start.4 = (bf16[512,512]{1,0:T(8,128)(2,1)S(1)}, bf16[512,512]{1,0:T(8,128)(2,1)}, u32[]{:S(2)}) copy-start(bf16[512,512]{1,0:T(8,128)(2,1)} %param.20) | copy-start | bytes 1572868
  23.2 107.1 %copy-start.5 = (bf16[512,512]{1,0:T(8,128)(2,1)S(1)}, bf16[512,512]{1,0:T(8,128)(2,1)}, u32[]{:S(2)}) copy-start(bf16[512,512]{1,0:T(8,128)(2,1)} %param.24) | copy-start | bytes 1572868
  23.2 107.6 %all-to-all-start = ((bf16[16,16,64,128]{3,2,1,0:T(8,128)(2,1)}), bf16[16,16,64,128]{3,2,1,0:T(8,128)(2,1)}, u32[]{:S(2)}, u32[]{:S(2)}) async-start(bf16[16,16,64,128]{3,2,1,0:T(8,128)(2,1)} %select_select_fusion), calls=%async_computation | async-start | bytes 8388608 | tf_op jit(solution)/shard_map/all_to_all | solution.py:69
  130.8 7.5 %copy-start.8 = (bf16[128,512]{1,0:T(8,128)(2,1)S(1)}, bf16[128,512]{1,0:T(8,128)(2,1)}, u32[]{:S(2)}) copy-start(bf16[128,512]{1,0:T(8,128)(2,1)} %param.22) | copy-start | bytes 393220
  130.8 7.5 %copy-start.9 = (f32[512]{0:T(512)S(1)}, f32[512]{0:T(512)}, u32[]{:S(2)}) copy-start(f32[512]{0:T(512)} %param.23) | copy-start | bytes 6148
  144.9 3.2 copy-start.11
  148.1 4.7 %copy-start.7 = (bf16[512,512]{1,0:T(8,128)(2,1)S(1)}, bf16[512,512]{1,0:T(8,128)(2,1)}, u32[]{:S(2)}) copy-start(bf16[512,512]{1,0:T(8,128)(2,1)} %param.25) | copy-start | bytes 1572868
  317.5 21.0 %copy-start.10 = (s32[64]{0:T(128)S(1)}, s32[64]{0:T(128)}, u32[]{:S(2)}) copy-start(s32[64]{0:T(128)} %param.31) | copy-start | bytes 772
  317.5 36.7 %copy-start.1 = (bf16[512,512]{1,0:T(8,128)(2,1)S(1)}, bf16[512,512]{1,0:T(8,128)(2,1)}, u32[]{:S(2)}) copy-start(bf16[512,512]{1,0:T(8,128)(2,1)} %param.26) | copy-start | bytes 1572868
  319.9 32.8 %all-to-all-start.1 = ((bf16[4,16,8,512]{3,2,0,1:T(8,128)(2,1)}), bf16[4,16,8,512]{3,2,0,1:T(8,128)(2,1)S(1)}, u32[]{:S(2)}, u32[]{:S(2)}) async-start(bf16[4,16,8,512]{3,2,0,1:T(8,128)(2,1)} %copy.20), calls=%async_computation.1 | async-start | bytes 1048576 | tf_op jit(solution)/shard_map/all_to_all | solution.py:131
where the time goes:
time: 358 us; the launch traced here: 354 us
  matrix products  116 us (32%)
  blocking collectives  95.8 us (27%)
  local copies, waits for them, and re-layouts  57.2 us (16%)
  starting transfers between devices  26.1 us (7%)
  other arithmetic  23 us (6%)
  loops' own time  21.6 us (6%)
  waiting for transfers between devices  14 us (4%)
    psum x1, blocking collectives, local(): lax.psum((jnp.sum(obs_wide, axis=0), jnp.sum(obs_wide * obs_wide, axis=0)...  95.8 us
    dot_general x32, matrix products, one_head(): lax.dot_general(query_head, key_head, (((1,), (1,)), ((), ())), preferred...  48.2 us
    dot_general x32, matrix products, one_head(): jnp.dot(weights_bf, value_head, preferred_element_type=jnp.float32) / totals  46.3 us
    another operation x4, loops' own time, local(): per_head = lax.map(one_head, jnp.arange(HEADS, dtype=jnp.int32))  21.6 us
    dynamic_slice x32, local copies, waits for them, and re-layouts, local(): per_head = lax.map(one_head, jnp.arange(HEADS, dtype=jnp.int32))  20 us
    all_to_all x1, starting transfers between devices, local(): lax.all_to_all(outgoing, 'tile', split_axis=1, concat_axis=0, tiled=True)  18.5 us
    all_to_all x1, waiting for transfers between devices, local(): lax.all_to_all(outgoing, 'tile', split_axis=1, concat_axis=0, tiled=True)  14 us
    gather x2, local copies, waits for them, and re-layouts, local(): spots = jnp.take(block_position, block_lists, axis=0)  13.3 us
  transfers between devices with their start and end apart: 2, of which 1 were waited for; matrix products, arithmetic and copies ran while one was open for 1% of the time, Pallas kernels for 0%

commit v1 on v0

--- a/solution.py
+++ b/solution.py
@@ -1,3 +1,4 @@
+import functools
 import jax
 import jax.numpy as jnp
 from jax import lax
@@ -7,6 +8,21 @@
 BLOCK = 64
 NSEL = 32
 TILE_ROWS = 128
+
+
+def register_signs(my_data, bus_axis, join_dim, in_dim):
+    return jnp.concatenate(
+        lax.all_to_all(
+            jnp.stack(jnp.split(my_data, lax.psum(1, axis_name=bus_axis), join_dim)),
+            axis_name=bus_axis,
+            split_axis=0,
+            concat_axis=0,
+        ),
+        in_dim,
+    )
+
+
+shape_the_tracks = functools.partial(register_signs, bus_axis="tile", join_dim=1, in_dim=0)
 
 
 def embed_rows(feats, feat_mean, feat_rstd, w_obs, b_obs):
@@ -128,7 +144,7 @@
     attended = jnp.concatenate(results, axis=0)
     encoded = jnp.dot(attended, w_out, preferred_element_type=jnp.float32).astype(jnp.bfloat16)
     outgoing = encoded.reshape(tile_local, tile_count, TILE_ROWS // tile_count, width)
-    arrived = lax.all_to_all(outgoing, "tile", split_axis=1, concat_axis=0, tiled=True)
+    arrived = shape_the_tracks(outgoing)
     arrived = arrived.reshape(tile_count * tile_local, TILE_ROWS // tile_count, width)
     return jnp.take(arrived, proc_order, axis=0).reshape(
         tile_count * tile_local * (TILE_ROWS // tile_count), width

time: 358 us -> 367 us (1.025)
  local copies, waits for them, and re-layouts: 57.2 us -> 66.2 us
    unnamed x25 -> x40, local copies, waits for them, and re-layouts: 4.12 us -> 13.4 us
where the time goes in v1:
time: 367 us; the launch traced here: 363 us
  matrix products  116 us (32%)
  blocking collectives  95.8 us (26%)
  local copies, waits for them, and re-layouts  66.2 us (18%)
  starting transfers between devices  26.1 us (7%)
  other arithmetic  23 us (6%)
  loops' own time  21.6 us (6%)
  waiting for transfers between devices  14 us (4%)
    psum x1, blocking collectives, local(): lax.psum((jnp.sum(obs_wide, axis=0), jnp.sum(obs_wide * obs_wide, axis=0)...  95.8 us
    dot_general x32, matrix products, one_head(): lax.dot_general(query_head, key_head, (((1,), (1,)), ((), ())), preferred...  48.2 us
    dot_general x32, matrix products, one_head(): jnp.dot(weights_bf, value_head, preferred_element_type=jnp.float32) / totals  46.3 us
    another operation x4, loops' own time, local(): per_head = lax.map(one_head, jnp.arange(HEADS, dtype=jnp.int32))  21.6 us
    dynamic_slice x32, local copies, waits for them, and re-layouts, local(): per_head = lax.map(one_head, jnp.arange(HEADS, dtype=jnp.int32))  20 us
    all_to_all x1, starting transfers between devices, register_signs(): lax.all_to_all(jnp.stack(jnp.split(my_data, lax.psum(1, axis_name=bus_axi...  18.5 us
    all_to_all x1, waiting for transfers between devices, register_signs(): lax.all_to_all(jnp.stack(jnp.split(my_data, lax.psum(1, axis_name=bus_axi...  14 us
    unnamed x40, local copies, waits for them, and re-layouts  13.4 us
  transfers between devices with their start and end apart: 2, of which 1 were waited for; matrix products, arithmetic and copies ran while one was open for 1% of the time, Pallas kernels for 0%

profile of v1, /device:TPU:0, one launch (start us, length us, event | category | flops | bytes accessed | tf_op | source)
XLA Modules:
  0.0 363.3 jit_solution(9890412594102539912)
XLA Ops:
  1.0 13.2 %gather_fusion = s32[2048]{0:T(1024)S(1)} fusion(s32[512]{0:T(512)S(1)} %copy-done.2, s32[2048]{0:T(1024)S(1)} %broadcast_clamp_fusion), kind=kCustom, calls=%fused_computation | custom fusion | bytes 24576 | tf_op jit(solution)/shard_map/jit(_take)/gather | solution.py:62
  16.2 3.1 gather_fusion.1
  19.3 3.9 %select_select_fusion = bf16[16,16,64,128]{3,2,1,0:T(8,128)(2,1)} fusion(bf16[16,16,64,128]{3,2,1,0:T(8,128)(2,1)} %bitcast.174, pred[16,16]{1,0:T(8,128)(4,1)S(1)} %compare_and_fusion, pred[16,16]{1,0:T(8,128)(4,1)S(1)} %fusion.75), kind=kLoop, calls=%fused_computation.76 | loop fusion | flops 4194304 | bytes 8389120 | tf_op jit(solution)/shard_map/jit(_where)/select_n | solution.py:86
  23.2 7.6 %all-to-all-start = ((bf16[16,16,64,128]{3,2,1,0:T(8,128)(2,1)}), bf16[16,16,64,128]{3,2,1,0:T(8,128)(2,1)}, u32[]{:S(2)}, u32[]{:S(2)}) async-start(bf16[16,16,64,128]{3,2,1,0:T(8,128)(2,1)} %select_select_fusion), calls=%async_computation | async-start | bytes 8388608 | tf_op jit(solution)/shard_map/all_to_all | solution.py:85
  31.4 95.8 %all-reduce = (f32[128]{0:T(128)S(1)}, f32[128]{0:T(128)S(1)}) all-reduce(f32[128]{0:T(128)S(1)} %get-tuple-element.226, f32[128]{0:T(128)S(1)} %get-tuple-element.225), channel_id=1, replica_groups=mesh['groups'=2,'tile'=16] {'tile'}, use_global_device_ids=true, to_apply=%region_6.7 | all-reduce | flops 256 | bytes 2048 | tf_op jit(solution)/shard_map/psum | solution.py:56
  130.8 3.2 gather_fusion.2
  134.0 4.3 %bitcast_select_fusion = bf16[8192,128]{1,0:T(8,128)(2,1)S(1)} fusion(bf16[128,64,128]{2,1,0:T(8,128)(2,1)S(1)} %gather_fusion.2, pred[8192]{0:T(1024)(128)(4,1)S(1)} %broadcast_in_dim.178), kind=kLoop, calls=%fused_computation.77 | loop fusion | flops 1048576 | bytes 4202496 | tf_op jit(solution)/shard_map/jit(_take)/select_n | solution.py:94
  138.3 6.6 %fusion.63 = bf16[8192,512]{1,0:T(8,128)(2,1)S(1)} fusion(bf16[128,512]{1,0:T(8,128)(2,1)S(1)} %copy-done.8, f32[512]{0:T(512)S(1)} %copy-done.9, bf16[8192,128]{1,0:T(8,128)(2,1)S(1)} %bitcast_select_fusion, f32[128]{0:T(128)S(1)} %get-tuple-element.315, f32[128]{0:T(128)S(1)} %get-tuple-element.314), kind=kOutput, calls=%fused_computation.72 | convolution fusion | flops 1119879168 | bytes 10619904 | tf_op jit(solution)/shard_map/dot_general | solution.py:30
  144.9 3.2 copy-done.11
  148.1 4.7 %convolution_convert_fusion = bf16[8192,512]{1,0:T(8,128)(2,1)S(1)} fusion(bf16[8192,512]{1,0:T(8,128)(2,1)S(1)} %fusion.63, bf16[512,512]{1,0:T(8,128)(2,1)S(1)} %copy-done), kind=kOutput, calls=%fused_computation.73 | convolution fusion | flops 4299161600 | bytes 17301504 | tf_op jit(solution)/shard_map/dot_general | solution.py:101
  152.9 8.1 %convolution_convert_fusion.1 = bf16[8192,512]{1,0:T(8,128)(2,1)S(1)} fusion(bf16[8192,512]{1,0:T(8,128)(2,1)} %copy-done.11, bf16[512,512]{1,0:T(8,128)(2,1)S(1)} %copy-done.7), kind=kOutput, calls=%fused_computation.74 | convolution fusion | flops 4299161600 | bytes 17301504 | tf_op jit(solution)/shard_map/dot_general | solution.py:100
  161.0 5.2 %fusion.102 = (bf16[2048,512]{1,0:T(8,128)(2,1)}, bf16[2048,512]{1,0:T(8,128)(2,1)S(1)}, bf16[2048,512]{1,0:T(8,128)(2,1)}, bf16[2048,512]{1,0:T(8,128)(2,1)}, b...) fusion(bf16[8192,512]{1,0:T(8,128)(2,1)S(1)} %convolution_conve, ...), kind=kLoop, calls=%fused_computation.172 | loop fusion | bytes 33554432 | tf_op jit(solution)/shard_map/slice | solution.py:115
  166.2 40.6 %while.44 = (s32[]{:T(128)}, bf16[8,128,64]{1,2,0:T(8,128)(2,1)S(1)}, s32[8]{0:T(128)S(1)}, bf16[128,512]{1,0:T(8,128)(2,1)S(1)}, bf16[2048,512]{1,0:T(8,128)(2,...) while((s32[]{:T(128)}, ...), condition=%wide.region_10.11_spmd.clone, body=%wide.region_7.10_spmd.clone.sunk | while | flops 68951808 | bytes 4272331 | solution.py:140
  169.6 1.7 fusion.138
  174.7 1.7 fusion.138
  184.8 1.7 fusion.138
  189.9 1.7 fusion.138
  194.9 1.7 fusion.138
  206.8 40.2 %while.45 = (s32[]{:T(128)}, bf16[8,128,64]{1,2,0:T(8,128)(2,1)S(1)}, s32[8]{0:T(128)S(1)}, bf16[128,512]{1,0:T(8,128)(2,1)S(1)}, bf16[2048,512]{1,0:T(8,128)(2,...) while((s32[]{:T(128)}, ...), condition=%wide.region_14.15_spmd.clone, body=%wide.region_11.14_spmd.clone.sunk | while | flops 68951808 | bytes 4272331 | solution.py:140
  210.1 1.7 fusion.143
  247.1 39.2 %while.46 = (s32[]{:T(128)}, bf16[8,128,64]{1,2,0:T(8,128)(2,1)S(1)}, s32[8]{0:T(128)S(1)}, bf16[128,512]{1,0:T(8,128)(2,1)S(1)}, bf16[2048,512]{1,0:T(8,128)(2,...) while((s32[]{:T(128)}, ...), condition=%wide.region_18.19_spmd.clone, body=%wide.region_15.18_spmd.clone.sunk | while | flops 68951808 | bytes 4272331 | solution.py:140
  250.5 1.7 fusion.148
  255.4 1.7 fusion.148
  260.2 1.7 fusion.148
  265.1 1.7 fusion.148
  270.0 1.7 fusion.148
  274.9 1.7 fusion.148
  279.7 1.7 fusion.148
  284.6 1.7 fusion.148
  286.4 31.1 %while.47 = (s32[]{:T(128)}, bf16[8,128,64]{1,2,0:T(8,128)(2,1)S(1)}, s32[8]{0:T(128)S(1)}, bf16[128,512]{1,0:T(8,128)(2,1)S(1)}, bf16[2048,512]{1,0:T(8,128)(2,...) while((s32[]{:T(128)}, ...), condition=%wide.region_22.23_spmd.clone, body=%wide.region_19.22_spmd.clone.sunk | while | flops 68951808 | bytes 4271823 | solution.py:140
  328.9 18.5 %all-to-all-start.1 = ((bf16[16,4,1,8,512]{4,3,1,2,0:T(8,128)(2,1)}), bf16[16,4,1,8,512]{4,3,1,2,0:T(8,128)(2,1)S(1)}, u32[]{:S(2)}, u32[]{:S(2)}) async-start(bf16[16,4,1,8,512]{4,3,1,2,0:T(8,128)(2,1)} %fusion.76), calls=%async_computation.1 | async-start | bytes 1048576 | tf_op jit(solution)/shard_map/all_to_all | solution.py:15
  347.7 14.0 %all-to-all-done.1 = bf16[16,4,1,8,512]{4,3,1,2,0:T(8,128)(2,1)S(1)} async-done(((bf16[16,4,1,8,512]{4,3,1,2,0:T(8,128)(2,1)}), bf16[16,4,1,8,512]{4,3,1,2,0:T(8,128)(2,1)S(1)}, u32[]{:S(2)}, u32[]{:S(2)}) %all-to-all-start.1) | async-done | bytes 524320 | tf_op jit(solution)/shard_map/all_to_all | solution.py:15
  (271 shorter events, 125.8 us)
Async XLA Ops:
  0.0 148.1 %copy-start = (bf16[512,512]{1,0:T(8,128)(2,1)S(1)}, bf16[512,512]{1,0:T(8,128)(2,1)}, u32[]{:S(2)}) copy-start(bf16[512,512]{1,0:T(8,128)(2,1)} %param.26) | copy-start | bytes 1572868
  0.0 1.0 copy-start.2
  1.0 13.4 %copy-start.6 = (s32[64]{0:T(128)S(1)}, s32[64]{0:T(128)}, u32[]{:S(2)}) copy-start(s32[64]{0:T(128)} %param.29) | copy-start | bytes 772
  1.0 15.2 %copy-start.3 = (bf16[2048,128]{1,0:T(8,128)(2,1)S(1)}, bf16[2048,128]{1,0:T(8,128)(2,1)}, u32[]{:S(2)}) copy-start(bf16[2048,128]{1,0:T(8,128)(2,1)} %param.21) | copy-start | bytes 1572868
  23.2 107.1 %copy-start.4 = (bf16[512,512]{1,0:T(8,128)(2,1)S(1)}, bf16[512,512]{1,0:T(8,128)(2,1)}, u32[]{:S(2)}) copy-start(bf16[512,512]{1,0:T(8,128)(2,1)} %param.20) | copy-start | bytes 1572868
  23.2 107.1 %copy-start.5 = (bf16[512,512]{1,0:T(8,128)(2,1)S(1)}, bf16[512,512]{1,0:T(8,128)(2,1)}, u32[]{:S(2)}) copy-start(bf16[512,512]{1,0:T(8,128)(2,1)} %param.24) | copy-start | bytes 1572868
  23.2 107.6 %all-to-all-start = ((bf16[16,16,64,128]{3,2,1,0:T(8,128)(2,1)}), bf16[16,16,64,128]{3,2,1,0:T(8,128)(2,1)}, u32[]{:S(2)}, u32[]{:S(2)}) async-start(bf16[16,16,64,128]{3,2,1,0:T(8,128)(2,1)} %select_select_fusion), calls=%async_computation | async-start | bytes 8388608 | tf_op jit(solution)/shard_map/all_to_all | solution.py:85
  130.8 7.5 %copy-start.8 = (bf16[128,512]{1,0:T(8,128)(2,1)S(1)}, bf16[128,512]{1,0:T(8,128)(2,1)}, u32[]{:S(2)}) copy-start(bf16[128,512]{1,0:T(8,128)(2,1)} %param.22) | copy-start | bytes 393220
  130.8 7.5 %copy-start.9 = (f32[512]{0:T(512)S(1)}, f32[512]{0:T(512)}, u32[]{:S(2)}) copy-start(f32[512]{0:T(512)} %param.23) | copy-start | bytes 6148
  144.9 3.2 copy-start.11
  148.1 4.7 %copy-start.7 = (bf16[512,512]{1,0:T(8,128)(2,1)S(1)}, bf16[512,512]{1,0:T(8,128)(2,1)}, u32[]{:S(2)}) copy-start(bf16[512,512]{1,0:T(8,128)(2,1)} %param.25) | copy-start | bytes 1572868
  317.5 30.0 %copy-start.10 = (s32[64]{0:T(128)S(1)}, s32[64]{0:T(128)}, u32[]{:S(2)}) copy-start(s32[64]{0:T(128)} %param.31) | copy-start | bytes 772
  317.5 45.8 %copy-start.1 = (bf16[512,512]{1,0:T(8,128)(2,1)S(1)}, bf16[512,512]{1,0:T(8,128)(2,1)}, u32[]{:S(2)}) copy-start(bf16[512,512]{1,0:T(8,128)(2,1)} %param.26) | copy-start | bytes 1572868
  328.9 32.8 %all-to-all-start.1 = ((bf16[16,4,1,8,512]{4,3,1,2,0:T(8,128)(2,1)}), bf16[16,4,1,8,512]{4,3,1,2,0:T(8,128)(2,1)S(1)}, u32[]{:S(2)}, u32[]{:S(2)}) async-start(bf16[16,4,1,8,512]{4,3,1,2,0:T(8,128)(2,1)} %fusion.76), calls=%async_computation.1 | async-start | bytes 1048576 | tf_op jit(solution)/shard_map/all_to_all | solution.py:15
